TPU v7x, 32 devices: a whole 2x2x4 slice. The times are simulated.
32 devices in a mesh: groups: 2 (over x), tm: 8 (over z, y), space: 2 (over core).
Axes of the slice: x: 2, y: 2, z: 4, core: 2. Of those that a mesh axis runs over, the one named last changes fastest.
Arguments:
- query_pre: bfloat16 [16, 8, 32, 2240], P(('groups', 'tm'), 'space'), parts along dimension 0, may hold values from -6 to 6
- key_pre: bfloat16 [16, 8, 32, 2240], P(('groups', 'tm'), 'space'), parts along dimension 0, may hold values from -6 to 6
- value_pre: bfloat16 [16, 8, 32, 2240], P(('groups', 'tm'), 'space'), parts along dimension 0, may hold values from -8 to 8
- grad_out: bfloat16 [16, 8, 32, 2240], P(('groups', 'tm'), 'space'), parts along dimension 0, may hold values from -96 to 96
- conv_taps: float32 [3, 3, 2240], replicated, may hold values from -4 to 4
Outputs:
- attended: bfloat16 [16, 8, 32, 2240], P(('groups', 'tm'), 'space'), parts along dimension 0
- query_grad: bfloat16 [16, 8, 32, 2240], P(('groups', 'tm'), 'space'), parts along dimension 0
- key_grad: bfloat16 [16, 8, 32, 2240], P(('groups', 'tm'), 'space'), parts along dimension 0
- value_grad: bfloat16 [16, 8, 32, 2240], P(('groups', 'tm'), 'space'), parts along dimension 0
- taps_grad: float32 [6, 3, 2240], P('groups'), parts along dimension 0
There are 2 independent parts, one for each index of `groups`. A program takes and returns all parts, laid end to end along the dimension named above; an argument that names none is the same for every part. Nothing has to cross between parts.
All inputs are finite; a program needn't handle non-finite values.
Results may differ from a plain program's by a relative error of at most 0.013.
Values may be sent and summed in bfloat16 or wider, within the bound.
A program may use at most 128 MiB of HBM per device.

v0:
```python
import jax
import jax.numpy as jnp
from jax import lax
from jax.sharding import PartitionSpec as P

HEADS = 20
HEAD_DIM = 112


def extended(block, sides, width):
    for axis, dim in sides:
        count = lax.axis_size(axis)
        forward = [(i, i + 1) for i in range(count - 1)]
        backward = [(target, source) for source, target in forward]
        low = lax.ppermute(
            lax.slice_in_dim(block, block.shape[dim] - width, None, axis=dim), axis, forward
        )
        high = lax.ppermute(lax.slice_in_dim(block, 0, width, axis=dim), axis, backward)
        block = jnp.concatenate([low, block, high], axis=dim)
    return block


def carried_in(part, axis, combine, identity):
    place = lax.axis_index(axis)
    gathered = jax.tree.map(lambda a: lax.all_gather(a, axis), part)
    state = jax.tree.map(lambda a, e: jnp.zeros_like(a) + jnp.asarray(e, a.dtype), part, identity)

    def one(turn, state):
        return combine(
            state, jax.tree.map(lambda a: lax.dynamic_index_in_dim(a, turn, 0, False), gathered)
        )

    return lax.fori_loop(0, place, one, state)


def carried_in_2(x, axis, join, neutral):
    count = lax.axis_size(axis)
    place = lax.axis_index(axis)
    ahead = count - 1 - place
    gathered = jax.tree.map(
        lambda a, kind: lax.all_gather(a.astype(kind), axis), x, (jnp.bfloat16, jnp.bfloat16)
    )
    state = jax.tree.map(lambda a, e: jnp.zeros_like(a) + jnp.asarray(e, a.dtype), x, neutral)

    def one(turn, state):
        source = count - 1 - turn
        return join(
            state,
            jax.tree.map(
                lambda a, own: lax.dynamic_index_in_dim(a, source, 0, False).astype(own.dtype),
                gathered,
                x,
            ),
        )

    return lax.fori_loop(0, ahead, one, state)


def mix_rows(padded, conv_taps, row_count, col_count, flipped):
    summed = jnp.zeros(padded.shape[:1] + (row_count, col_count, padded.shape[3]), jnp.float32)
    for row_off in range(3):
        for col_off in range(3):
            if flipped:
                window = padded[
                    :, 2 - row_off : 2 - row_off + row_count, 2 - col_off : 2 - col_off + col_count
                ]
            else:
                window = padded[:, row_off : row_off + row_count, col_off : col_off + col_count]
            summed = summed + conv_taps[row_off, col_off] * window
    return summed


def add_pair(earlier, later):
    return (earlier[0] + later[0], earlier[1] + later[1])


def shards(query_pre, key_pre, value_pre, grad_out, conv_taps):
    frame_count, row_count, col_count, model_width = value_pre.shape
    head_count = HEADS
    head_size = HEAD_DIM
    token_count = frame_count * row_count * col_count
    split = (token_count, head_count, head_size)
    highest = lax.Precision.HIGHEST
    value_rows, grad_band = (
        extended(value_pre, (("space", 1),), 1),
        extended(grad_out, (("space", 1),), 1),
    )
    value_pad = jnp.pad(value_rows, ((0, 0), (0, 0), (1, 1), (0, 0)))
    local = mix_rows(value_pad, conv_taps, row_count, col_count, False)
    queries = jnp.maximum(query_pre, 0).reshape(split)
    keys = jnp.maximum(key_pre, 0).reshape(split)
    values = value_pre.reshape(split)
    partial_value = jnp.einsum("the,thd->hed", keys, values, preferred_element_type=jnp.float32)
    key_sum = jnp.sum(keys, axis=0, dtype=jnp.float32)
    half_state, half_sum = (
        lax.psum_scatter(partial_value, "space", scatter_dimension=0, tiled=True),
        lax.psum_scatter(key_sum, "space", scatter_dimension=0, tiled=True),
    )
    before = carried_in(
        (half_state, half_sum),
        "tm",
        add_pair,
        (jnp.zeros_like(half_state), jnp.zeros_like(half_sum)),
    )
    kv_state, key_total = (
        lax.all_gather(before[0] + half_state, "space", axis=0, tiled=True),
        lax.all_gather(before[1] + half_sum, "space", axis=0, tiled=True),
    )
    query_f32 = queries.astype(jnp.float32)
    numerator = jnp.einsum("the,hed->thd", query_f32, kv_state, precision=highest)
    denominator = jnp.einsum("the,he->th", query_f32, key_total, precision=highest) + 1.0
    output_f32 = numerator / denominator[..., None]
    attended = (output_f32.reshape(value_pre.shape) + local).astype(jnp.bfloat16)
    cotangent = grad_out.astype(jnp.float32).reshape(split)
    grad_num = cotangent / denominator[..., None]
    grad_den = -jnp.sum(cotangent * output_f32, axis=-1) / denominator
    grad_query = (
        jnp.einsum("thd,hed->the", grad_num, kv_state, precision=highest)
        + grad_den[..., None] * key_total[None]
    )
    grad_partial = jnp.einsum("the,thd->hed", query_f32, grad_num, precision=highest)
    grad_keysum = jnp.einsum("th,the->he", grad_den, query_f32, precision=highest)
    half_grad, half_keysum = (
        lax.psum_scatter(grad_partial, "space", scatter_dimension=0, tiled=True),
        lax.psum_scatter(grad_keysum, "space", scatter_dimension=0, tiled=True),
    )
    after = carried_in_2(
        (half_grad, half_keysum),
        "tm",
        add_pair,
        (jnp.zeros_like(half_grad), jnp.zeros_like(half_keysum)),
    )
    grad_state, grad_total = (
        lax.all_gather(
            (after[0] + half_grad).astype(jnp.bfloat16), "space", axis=0, tiled=True
        ).astype(jnp.float32),
        lax.all_gather(
            (after[1] + half_keysum).astype(jnp.bfloat16), "space", axis=0, tiled=True
        ).astype(jnp.float32),
    )
    grad_key = (
        jnp.einsum("thd,hed->the", values.astype(jnp.float32), grad_state, precision=highest)
        + grad_total[None]
    )
    grad_mixed = jnp.einsum(
        "the,hed->thd", keys.astype(jnp.float32), grad_state, precision=highest
    ).reshape(value_pre.shape)
    query_grad = jnp.where(query_pre > 0, grad_query.reshape(value_pre.shape), 0.0).astype(
        jnp.bfloat16
    )
    key_grad = jnp.where(key_pre > 0, grad_key.reshape(value_pre.shape), 0.0).astype(jnp.bfloat16)
    grad_pad = jnp.pad(grad_band, ((0, 0), (0, 0), (1, 1), (0, 0)))
    value_grad = (grad_mixed + mix_rows(grad_pad, conv_taps, row_count, col_count, True)).astype(
        jnp.bfloat16
    )
    cotangent_full = grad_out.astype(jnp.float32)
    tap_rows = []
    for row_off in range(3):
        tap_cols = []
        for col_off in range(3):
            window = value_pad[:, row_off : row_off + row_count, col_off : col_off + col_count]
            tap_cols.append(jnp.sum(cotangent_full * window, axis=(0, 1, 2)))
        tap_rows.append(jnp.stack(tap_cols))
    taps_grad = lax.psum(jnp.stack(tap_rows), ("tm", "space"))
    return (attended, query_grad, key_grad, value_grad, taps_grad)


def solution(mesh):
    return jax.shard_map(
        shards,
        mesh=mesh,
        in_specs=(
            P(("groups", "tm"), "space", None, None),
            P(("groups", "tm"), "space", None, None),
            P(("groups", "tm"), "space", None, None),
            P(("groups", "tm"), "space", None, None),
            P(),
        ),
        out_specs=(
            P(("groups", "tm"), "space", None, None),
            P(("groups", "tm"), "space", None, None),
            P(("groups", "tm"), "space", None, None),
            P(("groups", "tm"), "space", None, None),
            P("groups", None, None),
        ),
        check_vma=False,
    )
```

profile of v0, /device:TPU:8, one launch (start us, length us, event | category | flops | bytes accessed | tf_op | source)
XLA Modules:
  0.0 254.5 jit_solution(9472925568814212947)
XLA Ops:
  8.0 1.1 broadcast_maximum_fusion.1
  9.2 0.8 reshape.70
  10.5 0.8 reshape.71
  11.8 1.5 fusion.43
  13.3 10.1 %reduce-scatter.7.cloned.1.call-done = f32[10,112,112]{2,1,0:T(8,128)} async-done(((f32[20,112,112]{2,1,0:T(8,128)}), f32[10,112,112]{2,1,0:T(8,128)}) %reduce-scatter.7.cloned.1.call-update) | async-done | bytes 501776 | tf_op jit(solution)/shard_map/reduce_scatter | solution.py:96
  23.7 2.7 %fusion = f32[16,112]{1,0:T(8,128)S(1)} fusion(f32[20,112]{1,0:T(8,128)S(1)} %reduce_sum.102), kind=kCustom, calls=%all-reduce-scatter | all-reduce-scatter fusion | flops 3585 | bytes 16640
  26.4 2.2 collective-permute-start.4
  28.7 0.9 broadcast_maximum_fusion
  29.5 0.7 reshape.74
  30.3 1.5 copy.42
  31.7 0.6 dynamic-slice.6
  33.0 2.0 reshape.72
  35.7 28.8 %all-gather.4 = f32[8,10,112]{2,1,0:T(8,128)S(1)} all-gather(f32[1,10,112]{2,1,0:T(8,128)S(1)} %fusion.37), channel_id=3, replica_groups=mesh['groups'=2,'tm'=8,'space'=2] {'tm'}, dimensions={0}, use_global_device_ids=true | all-gather | bytes 40320 | tf_op jit(solution)/shard_map/all_gather | solution.py:25
  64.5 39.8 %all-gather.11.cloned.1.call-done = f32[80,112,112]{2,1,0:T(8,128)} async-done(((f32[10,112,112]{2,1,0:T(8,128)}), f32[80,112,112]{2,1,0:T(8,128)}) %all-gather.11.cloned.1.call-update) | async-done | bytes 4014096 | tf_op jit(solution)/shard_map/all_gather | solution.py:25
  104.3 2.5 while.26
  104.4 1.3 bitcast_add_fusion.5
  105.7 1.2 bitcast_add_fusion.5
  106.9 0.7 add_bitcast_fusion
  107.6 1.8 all-gather.5
  110.0 2.4 fusion.33
  112.5 13.9 %reduce-scatter.9.cloned.1.call-done = f32[10,112,112]{2,1,0:T(8,128)} async-done(((f32[20,112,112]{2,1,0:T(8,128)}), f32[10,112,112]{2,1,0:T(8,128)}) %reduce-scatter.9.cloned.1.call-update) | async-done | bytes 501776 | tf_op jit(solution)/shard_map/reduce_scatter | solution.py:124
  126.4 1.8 convert_element_type.134
  128.3 1.3 collective-permute-start.1
  129.6 3.0 %collective-permute-start = (bf16[1,1,32,2240]{3,2,1,0:T(8,128)(2,1)S(1)}, bf16[1,1,32,2240]{3,2,1,0:T(8,128)(2,1)S(1)}, u32[]{:S(2)}, u32[]{:S(2)}) collective-permute-start(bf16[1,1,32,2240]{3,2,1,0:T(8,128)(2,1)S(1)} %get-tuple-element.171), channel_id=1, source_target_pairs={{0,1},{2,3},{4,5},{6,7},{8,9},{10,11},{12,13},{14,15},{16,17},{18,... | collective-permute-start | bytes 430088 | tf_op jit(solution)/shard_map/ppermute | solution.py:15
  132.6 0.7 fusion.41
  133.4 1.3 collective-permute-start.3
  134.7 3.7 %collective-permute-start.2 = (bf16[1,1,32,2240]{3,2,1,0:T(8,128)(2,1)}, bf16[1,1,32,2240]{3,2,1,0:T(8,128)(2,1)}, u32[]{:S(2)}, u32[]{:S(2)}) collective-permute-start(bf16[1,1,32,2240]{3,2,1,0:T(8,128)(2,1)} %get-tuple-element.169), channel_id=1, source_target_pairs={{0,1},{2,3},{4,5},{6,7},{8,9},{10,11},{12,13},{14,15},{16,17},{18,... | collective-permute-start | bytes 430088 | tf_op jit(solution)/shard_map/ppermute | solution.py:15
  138.4 0.8 slice_reduce_fusion.8
  139.5 1.1 fusion.23
  140.9 0.7 pad_maximum_fusion.4
  141.6 0.7 copy-done.20
  142.3 1.5 select_maximum_fusion
  143.8 0.6 reshape.87
  144.4 1.1 add.145
  145.5 2.9 %all_gather.40 = f32[20,112,112]{2,1,0:T(8,128)S(1)} all-gather(f32[10,112,112]{2,1,0:T(8,128)S(1)} %add.145), channel_id=1, replica_groups=mesh['groups'=2,'tm'=8,'space'=2] {'space'}, dimensions={0}, use_global_device_ids=true | all-gather | bytes 1505280 | tf_op jit(solution)/shard_map/all_gather | solution.py:106
  148.5 2.7 %multiply_reduce_fusion = (f32[128,20]{0,1:T(8,128)}, f32[128,20,112]{0,2,1:T(8,128)}) fusion(f32[128,20,112]{0,2,1:T(8,128)S(1)} %copy-done.18, f32[128,20]{0,1:T(8,128)S(1)} %copy-done.37, f32[20,112,112]{2,1,0:T(8,128)S(1)} %all_gather.40, bf16[128,20,112]{0,2,1:T(8,128)(2,1)S(1)} %copy-done.10), kind=kOutput, calls=%fused_computation.62 | convolution fusion | flops 386209280 | bytes 3891200 | tf_op jit(solution)/shard_map/the,hed->thd/dot_general | solution.py:110
  151.2 2.9 %copy.41 = f32[128,20,112]{2,1,0:T(8,128)} copy(f32[128,20,112]{0,2,1:T(8,128)} %get-tuple-element.174) | data formatting | bytes 2293760 | tf_op jit(solution)/shard_map/div | solution.py:112
  154.2 2.7 %reshape.73 = f32[1,4,32,2240]{3,2,1,0:T(8,128)} reshape(f32[128,20,112]{2,1,0:T(8,128)} %copy.41) | data formatting | bytes 2293760 | tf_op jit(solution)/shard_map/reshape | solution.py:113
  156.9 0.7 negate_divide_fusion
  157.6 1.0 fusion.35
  158.6 2.7 %fusion.1 = f32[16,112]{1,0:T(8,128)S(1)} fusion(f32[20,112]{1,0:T(8,128)S(1)} %bitcast.88), kind=kCustom, calls=%all-reduce-scatter.1 | all-reduce-scatter fusion | flops 3585 | bytes 16640
  161.3 2.2 collective-permute-start.5
  163.6 3.3 %fusion.15 = bf16[1,4,32,2240]{3,2,1,0:T(8,128)(2,1)} fusion(f32[1,4,32,2240]{3,2,1,0:T(8,128)} %reshape.73, bf16[1,4,32,2240]{3,2,1,0:T(8,128)(2,1)S(1)} %copy-done, bf16[1,1,32,2240]{3,2,1,0:T(8,128)(2,1)S(1)} %collective-permute-done.1, bf16[1,1,32,2240]{3,2,1,0:T(8,128)(2,1)} %copy-done.14, f32[2240]{0:T(1024)} %get-tuple-element.143, ...), kind=kLoop, calls=%fused_computation.42 | loop fusion | flops 8601600 | bytes 6101760 | tf_op jit(solution)/shard_map/convert_element_type | solution.py:113
  166.9 1.4 fusion.5
  168.8 1.4 reshape.75
  170.3 28.0 %all-gather.6 = bf16[8,10,112]{2,1,0:T(8,128)(2,1)S(1)} all-gather(bf16[1,10,112]{2,1,0:T(8,128)(2,1)S(1)} %fusion.39), channel_id=5, replica_groups=mesh['groups'=2,'tm'=8,'space'=2] {'tm'}, dimensions={0}, use_global_device_ids=true | all-gather | bytes 20160 | tf_op jit(solution)/shard_map/all_gather | solution.py:41
  198.4 5.6 %while.27 = (s32[]{:T(128)}, f32[10,112,112]{2,1,0:T(8,128)S(1)}, f32[10,112]{1,0:T(8,128)S(1)}, s32[]{:T(128)}, bf16[8,10,112,112]{3,2,1,0:T(8,128)(2,1)}, /*in...) while((s32[]{:T(128)}, f32[10,112,112]{2,1,0:T(8,128)S(1)}, ...), condition=%wide.region_9.10_spmd, body=%wide.region_8.9_spmd.sunk | while | flops 253126 | bytes 1265763 | solution.py:56
  198.4 1.1 convert_add_fusion.4
  199.6 1.1 convert_add_fusion.4
  200.7 1.1 convert_add_fusion.4
  201.8 1.1 convert_add_fusion.4
  202.9 1.1 convert_add_fusion.4
  204.1 2.3 all_gather.46
  206.5 1.9 all-gather.7
  208.5 1.4 convolution_bitcast_fusion
  209.8 1.3 fusion.3
  211.1 1.6 copy.47
  212.7 1.4 reshape.76
  214.1 1.6 copy.50
  215.7 1.9 reshape.77
  217.7 2.8 %select_convert_fusion = (bf16[1,4,32,2240]{3,2,1,0:T(8,128)(2,1)}, bf16[1,4,32,2240]{3,2,1,0:T(8,128)(2,1)}) fusion(bf16[1,4,32,2240]{3,2,1,0:T(8,128)(2,1)} %reshape.76, bf16[1,4,32,2240]{3,2,1,0:T(8,128)(2,1)S(1)} %copy-done.4, bf16[1,4,32,2240]{3,2,1,0:T(8,128)(2,1)} %reshape.75, bf16[1,4,32,2240]{3,2,1,0:T(8,128)(2,1)} %param.9), kind=kLoop, calls=%fused_computation.59 | loop fusion | flops 2007040 | bytes 3440640 | tf_op jit(solution)/shard_map/convert_element_type | solution.py:151
  220.6 2.7 %fusion.22 = bf16[1,4,32,2240]{3,2,1,0:T(8,128)(2,1)} fusion(f32[1,4,32,2240]{3,2,1,0:T(8,128)S(1)} %reshape.77, bf16[1,4,32,2240]{3,2,1,0:T(8,128)(2,1)S(1)} %copy-done.2, bf16[1,6,34,2240]{3,2,1,0:T(8,128)(2,1)S(1)} %select_maximum_fusion, bf16[1,1,32,2240]{3,2,1,0:T(8,128)(2,1)} %collective-permute-done.2, bf16[1,1,32,2240]{3,2,1,0:T(8,128)(2,1)S(1)} %copy-done.21, ...), kind=kLoop, calls=%fused_computation.49 | loop fusion | flops 8601600 | bytes 6101760 | tf_op jit(solution)/shard_map/convert_element_type | solution.py:153
  223.3 22.5 %all-reduce.8.cloned.1.call-done = f32[3,3,2240]{2,1,0:T(4,128)} async-done(((f32[3,3,2240]{2,1,0:T(4,128)}), f32[3,3,2240]{2,1,0:T(4,128)}) %all-reduce.8.cloned.1.call-update) | async-done | bytes 80656 | tf_op jit(solution)/shard_map/psum | solution.py:164
  245.8 1.6 copy.83
  (139 shorter events, 4.2 us)
Async XLA Ops:
  8.0 15.4 %reduce-scatter.7.cloned.1.call-start = ((), (), s32[]{:S(2)}) async-start(), calls=%async_computation.2 | async-start | bytes 1720320 | tf_op jit(solution)/shard_map/reduce_scatter | solution.py:96
  9.2 1.3 copy-start
  10.5 1.3 copy-start.5
  11.8 1.5 copy-start.7
  13.3 10.3 %copy-start.3 = (bf16[1,4,32,2240]{3,2,1,0:T(8,128)(2,1)S(1)}, bf16[1,4,32,2240]{3,2,1,0:T(8,128)(2,1)}, u32[]{:S(2)}) copy-start(bf16[1,4,32,2240]{3,2,1,0:T(8,128)(2,1)} %param.10) | copy-start | bytes 1720324
  13.3 15.4 %copy-start.12 = (bf16[1,4,32,2240]{3,2,1,0:T(8,128)(2,1)S(1)}, bf16[1,4,32,2240]{3,2,1,0:T(8,128)(2,1)}, u32[]{:S(2)}) copy-start(bf16[1,4,32,2240]{3,2,1,0:T(8,128)(2,1)} %param.9) | copy-start | bytes 1720324
  13.3 91.0 %all-gather.11.cloned.1.call-start = ((), (), s32[]{:S(2)}) async-start(), calls=%async_computation.5 | async-start | bytes 5160960 | tf_op jit(solution)/shard_map/all_gather | solution.py:25
  23.4 6.1 %copy-start.1 = (bf16[1,4,32,2240]{3,2,1,0:T(8,128)(2,1)S(1)}, bf16[1,4,32,2240]{3,2,1,0:T(8,128)(2,1)}, u32[]{:S(2)}) copy-start(bf16[1,4,32,2240]{3,2,1,0:T(8,128)(2,1)} %param.12) | copy-start | bytes 1720324
  23.5 102.9 %reduce-scatter.9.cloned.1.call-start = ((), (), s32[]{:S(2)}) async-start(), calls=%async_computation.3 | async-start | bytes 1720320 | tf_op jit(solution)/shard_map/reduce_scatter | solution.py:124
  26.4 9.1 %collective-permute-start.4 = (f32[6,112]{1,0:T(8,128)S(1)}, f32[6,112]{1,0:T(8,128)S(1)}, u32[]{:S(2)}, u32[]{:S(2)}) collective-permute-start(f32[6,112]{1,0:T(8,128)S(1)} %slice.158), channel_id=1, source_target_pairs={{0,1},{2,3},{4,5},{6,7},{8,9},{10,11},{12,13},{14,15},{16,17},{18,... | collective-permute-start | bytes 8072
  30.3 1.5 copy-start.39
  35.5 74.5 %copy-start.9 = (bf16[128,20,112]{0,2,1:T(8,128)(2,1)}, bf16[128,20,112]{0,2,1:T(8,128)(2,1)S(1)}, u32[]{:S(2)}) copy-start(bf16[128,20,112]{0,2,1:T(8,128)(2,1)S(1)} %copy.40) | copy-start | bytes 1720324
  35.7 68.6 %copy-start.31 = (f32[22,112]{1,0:T(8,128)}, f32[22,112]{1,0:T(8,128)S(1)}, u32[]{:S(2)}) copy-start(f32[22,112]{1,0:T(8,128)S(1)} %concatenate.24) | copy-start | bytes 29572
  104.3 5.7 %copy-start.17 = (f32[128,20,112]{0,2,1:T(8,128)S(1)}, f32[128,20,112]{0,2,1:T(8,128)}, u32[]{:S(2)}) copy-start(f32[128,20,112]{0,2,1:T(8,128)} %copy.42) | copy-start | bytes 3440644
  110.0 2.4 copy-start.30
  110.0 2.4 copy-start.36
  112.4 26.0 %copy-start.32 = (f32[3,3,2240]{2,1,0:T(4,128)S(1)}, f32[3,3,2240]{2,1,0:T(4,128)}, u32[]{:S(2)}) copy-start(f32[3,3,2240]{2,1,0:T(4,128)} %param.13) | copy-start | bytes 241924
  112.4 85.9 %all-gather.13.cloned.1.call-start = ((), (), s32[]{:S(2)}) async-start(), calls=%async_computation.6 | async-start | bytes 2580480 | tf_op jit(solution)/shard_map/all_gather | solution.py:41
  128.2 117.6 %all-reduce.8.cloned.1.call-start = ((), (), s32[]{:S(2)}) async-start(), calls=%async_computation.4 | async-start | bytes 221184 | tf_op jit(solution)/shard_map/psum | solution.py:164
  128.3 10.9 %collective-permute-start.1 = (bf16[1,1,32,2240]{3,2,1,0:T(8,128)(2,1)S(1)}, bf16[1,1,32,2240]{3,2,1,0:T(8,128)(2,1)S(1)}, u32[]{:S(2)}, u32[]{:S(2)}) collective-permute-start(bf16[1,1,32,2240]{3,2,1,0:T(8,128)(2,1)S(1)} %get-tuple-element.172), channel_id=1, source_target_pairs={{1,0},{3,2},{5,4},{7,6},{9,8},{11,10},{13,12},{15,14},{17,16},{19,... | collective-permute-start | bytes 430088 | tf_op jit(solution)/shard_map/ppermute | solution.py:18
  129.6 9.6 %collective-permute-start = (bf16[1,1,32,2240]{3,2,1,0:T(8,128)(2,1)S(1)}, bf16[1,1,32,2240]{3,2,1,0:T(8,128)(2,1)S(1)}, u32[]{:S(2)}, u32[]{:S(2)}) collective-permute-start(bf16[1,1,32,2240]{3,2,1,0:T(8,128)(2,1)S(1)} %get-tuple-element.171), channel_id=1, source_target_pairs={{0,1},{2,3},{4,5},{6,7},{8,9},{10,11},{12,13},{14,15},{16,17},{18,... | collective-permute-start | bytes 430088 | tf_op jit(solution)/shard_map/ppermute | solution.py:15
  133.4 8.2 %collective-permute-start.3 = (bf16[1,1,32,2240]{3,2,1,0:T(8,128)(2,1)}, bf16[1,1,32,2240]{3,2,1,0:T(8,128)(2,1)S(1)}, u32[]{:S(2)}, u32[]{:S(2)}) collective-permute-start(bf16[1,1,32,2240]{3,2,1,0:T(8,128)(2,1)} %get-tuple-element.170), channel_id=1, source_target_pairs={{1,0},{3,2},{5,4},{7,6},{9,8},{11,10},{13,12},{15,14},{17,16},{19,... | collective-permute-start | bytes 430088 | tf_op jit(solution)/shard_map/ppermute | solution.py:18
  134.7 7.6 %collective-permute-start.2 = (bf16[1,1,32,2240]{3,2,1,0:T(8,128)(2,1)}, bf16[1,1,32,2240]{3,2,1,0:T(8,128)(2,1)}, u32[]{:S(2)}, u32[]{:S(2)}) collective-permute-start(bf16[1,1,32,2240]{3,2,1,0:T(8,128)(2,1)} %get-tuple-element.169), channel_id=1, source_target_pairs={{0,1},{2,3},{4,5},{6,7},{8,9},{10,11},{12,13},{14,15},{16,17},{18,... | collective-permute-start | bytes 430088 | tf_op jit(solution)/shard_map/ppermute | solution.py:15
  139.2 1.5 copy-start.14
  141.6 0.7 copy-start.20
  144.4 4.1 %copy-start.37 = (f32[128,20]{0,1:T(8,128)S(1)}, f32[128,20]{0,1:T(8,128)}, u32[]{:S(2)}) copy-start(f32[128,20]{0,1:T(8,128)} %copy-done.36) | copy-start | bytes 30724
  145.5 3.0 %copy-start.10 = (bf16[128,20,112]{0,2,1:T(8,128)(2,1)S(1)}, bf16[128,20,112]{0,2,1:T(8,128)(2,1)}, u32[]{:S(2)}) copy-start(bf16[128,20,112]{0,2,1:T(8,128)(2,1)} %copy-done.9) | copy-start | bytes 1720324
  145.5 3.0 %copy-start.18 = (f32[128,20,112]{0,2,1:T(8,128)S(1)}, f32[128,20,112]{0,2,1:T(8,128)}, u32[]{:S(2)}) copy-start(f32[128,20,112]{0,2,1:T(8,128)} %copy.42) | copy-start | bytes 3440644
  148.5 2.7 %copy-start.15 = (f32[20,112,112]{2,1,0:T(8,128)}, f32[20,112,112]{2,1,0:T(8,128)S(1)}, u32[]{:S(2)}) copy-start(f32[20,112,112]{2,1,0:T(8,128)S(1)} %all_gather.40) | copy-start | bytes 3010564
  154.1 9.4 %copy-start.22 = (f32[2240]{0:T(1024)S(1)}, f32[2240]{0:T(1024)}, u32[]{:S(2)}) copy-start(f32[2240]{0:T(1024)} %get-tuple-element.137) | copy-start | bytes 26884
  157.6 1.0 copy-start.33
  161.3 8.9 %collective-permute-start.5 = (f32[6,112]{1,0:T(8,128)S(1)}, f32[6,112]{1,0:T(8,128)S(1)}, u32[]{:S(2)}, u32[]{:S(2)}) collective-permute-start(f32[6,112]{1,0:T(8,128)S(1)} %slice.159), channel_id=1, source_target_pairs={{0,1},{2,3},{4,5},{6,7},{8,9},{10,11},{12,13},{14,15},{16,17},{18,... | collective-permute-start | bytes 8072
  163.5 3.4 %copy-start.16 = (f32[20,112,112]{2,1,0:T(8,128)S(1)}, f32[20,112,112]{2,1,0:T(8,128)}, u32[]{:S(2)}) copy-start(f32[20,112,112]{2,1,0:T(8,128)} %copy-done.15) | copy-start | bytes 3010564
  163.5 3.4 %copy-start.19 = (f32[128,20,112]{0,2,1:T(8,128)S(1)}, f32[128,20,112]{0,2,1:T(8,128)}, u32[]{:S(2)}) copy-start(f32[128,20,112]{0,2,1:T(8,128)} %copy.42) | copy-start | bytes 3440644
  163.5 3.4 %copy-start.34 = (f32[128,20]{0,1:T(8,128)S(1)}, f32[128,20]{0,1:T(8,128)}, u32[]{:S(2)}) copy-start(f32[128,20]{0,1:T(8,128)} %copy-done.33) | copy-start | bytes 30724
  163.6 3.4 %copy-start.35 = (f32[20,112]{1,0:T(8,128)S(1)}, f32[20,112]{1,0:T(8,128)}, u32[]{:S(2)}) copy-start(f32[20,112]{1,0:T(8,128)} %reshape.87) | copy-start | bytes 26884
  163.6 3.4 %copy-start.38 = (f32[128,20]{0,1:T(8,128)S(1)}, f32[128,20]{0,1:T(8,128)}, u32[]{:S(2)}) copy-start(f32[128,20]{0,1:T(8,128)} %copy-done.36) | copy-start | bytes 30724
  198.4 5.6 %copy-start.13 = (f32[10,112,112]{2,1,0:T(8,128)S(1)}, f32[10,112,112]{2,1,0:T(8,128)}, u32[]{:S(2)}) copy-start(f32[10,112,112]{2,1,0:T(8,128)} %reduce-scatter.9.cloned.1.call-done) | copy-start | bytes 1505284
  204.0 4.4 %copy-start.6 = (bf16[128,20,112]{0,2,1:T(8,128)(2,1)S(1)}, bf16[128,20,112]{0,2,1:T(8,128)(2,1)}, u32[]{:S(2)}) copy-start(bf16[128,20,112]{0,2,1:T(8,128)(2,1)} %copy-done.5) | copy-start | bytes 1720324
  206.5 3.4 %copy-start.8 = (bf16[128,20,112]{0,2,1:T(8,128)(2,1)S(1)}, bf16[128,20,112]{0,2,1:T(8,128)(2,1)}, u32[]{:S(2)}) copy-start(bf16[128,20,112]{0,2,1:T(8,128)(2,1)} %copy-done.7) | copy-start | bytes 1720324
  211.1 3.0 %copy-start.11 = (f32[128,20,112]{0,2,1:T(8,128)S(1)}, f32[128,20,112]{0,2,1:T(8,128)}, u32[]{:S(2)}) copy-start(f32[128,20,112]{0,2,1:T(8,128)} %convolution_bitcast_fusion) | copy-start | bytes 3440644
  215.7 1.9 copy-start.4
  217.6 2.9 %copy-start.2 = (bf16[1,4,32,2240]{3,2,1,0:T(8,128)(2,1)S(1)}, bf16[1,4,32,2240]{3,2,1,0:T(8,128)(2,1)}, u32[]{:S(2)}) copy-start(bf16[1,4,32,2240]{3,2,1,0:T(8,128)(2,1)} %param.12) | copy-start | bytes 1720324
  217.6 2.9 %copy-start.21 = (bf16[1,1,32,2240]{3,2,1,0:T(8,128)(2,1)S(1)}, bf16[1,1,32,2240]{3,2,1,0:T(8,128)(2,1)}, u32[]{:S(2)}) copy-start(bf16[1,1,32,2240]{3,2,1,0:T(8,128)(2,1)} %copy-done.20) | copy-start | bytes 430084
  217.6 2.9 %copy-start.23 = (f32[2240]{0:T(1024)S(1)}, f32[2240]{0:T(1024)}, u32[]{:S(2)}) copy-start(f32[2240]{0:T(1024)} %get-tuple-element.138) | copy-start | bytes 26884
  217.7 2.9 %copy-start.24 = (f32[2240]{0:T(1024)S(1)}, f32[2240]{0:T(1024)}, u32[]{:S(2)}) copy-start(f32[2240]{0:T(1024)} %get-tuple-element.139) | copy-start | bytes 26884
  217.7 2.9 %copy-start.25 = (f32[2240]{0:T(1024)S(1)}, f32[2240]{0:T(1024)}, u32[]{:S(2)}) copy-start(f32[2240]{0:T(1024)} %get-tuple-element.140) | copy-start | bytes 26884
  217.7 2.9 %copy-start.26 = (f32[2240]{0:T(1024)S(1)}, f32[2240]{0:T(1024)}, u32[]{:S(2)}) copy-start(f32[2240]{0:T(1024)} %get-tuple-element.141) | copy-start | bytes 26884
  217.7 2.9 %copy-start.27 = (f32[2240]{0:T(1024)S(1)}, f32[2240]{0:T(1024)}, u32[]{:S(2)}) copy-start(f32[2240]{0:T(1024)} %get-tuple-element.142) | copy-start | bytes 26884
  217.7 2.9 %copy-start.28 = (f32[2240]{0:T(1024)S(1)}, f32[2240]{0:T(1024)}, u32[]{:S(2)}) copy-start(f32[2240]{0:T(1024)} %get-tuple-element.143) | copy-start | bytes 26884
  217.7 2.9 %copy-start.29 = (f32[2240]{0:T(1024)S(1)}, f32[2240]{0:T(1024)}, u32[]{:S(2)}) copy-start(f32[2240]{0:T(1024)} %get-tuple-element.144) | copy-start | bytes 26884
Sparse Core Ops, SparseCore 0:
  13.4 9.9 reduce-scatter.6
  25.6 78.6 all-gather.10
  112.5 13.7 reduce-scatter.8
  128.4 52.3 all-gather.12
Sparse Core Ops, SparseCore 1:
  141.7 104.1 all-reduce.7
where the time goes:
time: 256 us; the launch traced here: 255 us
  waiting for transfers between devices  86.4 us (34%)
  blocking collectives  71.2 us (28%)
  other arithmetic  27.1 us (11%)
  local copies, waits for them, and re-layouts  26.9 us (11%)
  between operations  16.6 us (6%)
  starting transfers between devices  14 us (5%)
  matrix products  12.1 us (5%)
    all_gather x1, waiting for transfers between devices, carried_in(): gathered = jax.tree.map(lambda a: lax.all_gather(a, axis), part)  39.8 us
    all_gather x1, blocking collectives, carried_in(): gathered = jax.tree.map(lambda a: lax.all_gather(a, axis), part)  28.8 us
    all_gather x1, blocking collectives, carried_in_2(): lax.all_gather(a.astype(kind), axis)  28 us
    psum x1, waiting for transfers between devices, shards(): taps_grad = lax.psum(jnp.stack(tap_rows), ('tm', 'space'))  22.5 us
    reduce_scatter x1, waiting for transfers between devices, shards(): lax.psum_scatter(grad_partial, 'space', scatter_dimension=0, tiled=True)  13.9 us
    reduce_scatter x1, waiting for transfers between devices, shards(): lax.psum_scatter(partial_value, 'space', scatter_dimension=0, tiled=True)  10.1 us
    add x14, other arithmetic, add_pair(): return (earlier[0] + later[0], earlier[1] + later[1])  7.9 us
    ppermute x2, starting transfers between devices, extended(): lax.ppermute(lax.slice_in_dim(block, block.shape[dim] - width, None, axis...  6.74 us
  transfers between devices with their start and end apart: 11, of which 4 were waited for; matrix products, arithmetic and copies ran while one was open for 22% of the time, Pallas kernels for 0%

commit v1 on v0

--- a/solution.py
+++ b/solution.py
@@ -161,7 +161,8 @@
             window = value_pad[:, row_off : row_off + row_count, col_off : col_off + col_count]
             tap_cols.append(jnp.sum(cotangent_full * window, axis=(0, 1, 2)))
         tap_rows.append(jnp.stack(tap_cols))
-    taps_grad = lax.psum(jnp.stack(tap_rows), ("tm", "space"))
+    half = lax.psum(jnp.stack(tap_rows), "space")
+    taps_grad = lax.psum(half, "tm")
     return (attended, query_grad, key_grad, value_grad, taps_grad)
 
 

time: 256 us -> 285 us (1.11)
  waiting for transfers between devices: 86.4 us -> 115 us
    psum x1 -> x2, waiting for transfers between devices: 22.5 us -> 58.1 us  [the longest x1 46.1 us: shards(): taps_grad = lax.psum(half, 'tm')]
    reduce_scatter x1, waiting for transfers between devices: 13.9 us -> 6.04 us  [shards(): lax.psum_scatter(grad_partial, 'space', scatter_dimension=0, tiled=True)]
  transfers between devices with their start and end apart: 11 -> 12, of which waited for: 4 -> 6; matrix products, arithmetic and copies ran while one was open for 22% -> 20% of each run, Pallas kernels for 0% -> 0%
where the time goes in v1:
time: 285 us; the launch traced here: 283 us
  waiting for transfers between devices  115 us (40%)
  blocking collectives  71.6 us (25%)
  local copies, waits for them, and re-layouts  27.5 us (10%)
  other arithmetic  25.7 us (9%)
  between operations  15.5 us (5%)
  starting transfers between devices  14 us (5%)
  matrix products  13.4 us (5%)
    psum x1, waiting for transfers between devices, shards(): taps_grad = lax.psum(half, 'tm')  46.1 us
    all_gather x1, waiting for transfers between devices, carried_in(): gathered = jax.tree.map(lambda a: lax.all_gather(a, axis), part)  39.8 us
    all_gather x1, blocking collectives, carried_in(): gathered = jax.tree.map(lambda a: lax.all_gather(a, axis), part)  28.8 us
    all_gather x1, blocking collectives, carried_in_2(): lax.all_gather(a.astype(kind), axis)  28.4 us
    psum x1, waiting for transfers between devices, shards(): half = lax.psum(jnp.stack(tap_rows), 'space')  11.9 us
    reduce_scatter x1, waiting for transfers between devices, shards(): lax.psum_scatter(partial_value, 'space', scatter_dimension=0, tiled=True)  10.1 us
    add x14, other arithmetic, add_pair(): return (earlier[0] + later[0], earlier[1] + later[1])  7.81 us
    ppermute x2, starting transfers between devices, extended(): lax.ppermute(lax.slice_in_dim(block, block.shape[dim] - width, None, axis...  6.74 us
  transfers between devices with their start and end apart: 12, of which 6 were waited for; matrix products, arithmetic and copies ran while one was open for 20% of the time, Pallas kernels for 0%

profile of v1, /device:TPU:8, one launch (start us, length us, event | category | flops | bytes accessed | tf_op | source)
XLA Modules:
  0.0 283.0 jit_solution(12367902203266790285)
XLA Ops:
  7.2 1.1 broadcast_maximum_fusion.1
  8.3 0.8 reshape.70
  9.6 0.8 reshape.71
  11.0 0.8 copy-done.6
  11.8 1.5 fusion.43
  13.3 10.1 %reduce-scatter.7.cloned.1.call-done = f32[10,112,112]{2,1,0:T(8,128)} async-done(((f32[20,112,112]{2,1,0:T(8,128)}), f32[10,112,112]{2,1,0:T(8,128)}) %reduce-scatter.7.cloned.1.call-update) | async-done | bytes 501776 | tf_op jit(solution)/shard_map/reduce_scatter | solution.py:96
  23.7 2.7 fusion
  26.4 2.2 collective-permute-start.4
  28.7 0.8 reshape.74
  29.5 1.5 copy.42
  32.2 1.7 reshape.72
  33.9 1.6 copy.40
  35.7 28.8 %all-gather.4 = f32[8,10,112]{2,1,0:T(8,128)S(1)} all-gather(f32[1,10,112]{2,1,0:T(8,128)S(1)} %fusion.37), channel_id=3, replica_groups=mesh['groups'=2,'tm'=8,'space'=2] {'tm'}, dimensions={0}, use_global_device_ids=true | all-gather | bytes 40320 | tf_op jit(solution)/shard_map/all_gather | solution.py:25
  64.5 39.8 %all-gather.11.cloned.1.call-done = f32[80,112,112]{2,1,0:T(8,128)} async-done(((f32[10,112,112]{2,1,0:T(8,128)}), f32[80,112,112]{2,1,0:T(8,128)}) %all-gather.11.cloned.1.call-update) | async-done | bytes 4014096 | tf_op jit(solution)/shard_map/all_gather | solution.py:25
  104.3 2.4 while.26
  104.3 1.2 bitcast_add_fusion.5
  105.5 1.2 bitcast_add_fusion.5
  106.8 1.8 all-gather.5
  109.2 3.6 %fusion.33 = f32[20,112,112]{2,1,0:T(8,128)} fusion(bf16[128,20,112]{0,2,1:T(8,128)(2,1)S(1)} %copy.40, f32[128,20,112]{0,2,1:T(8,128)} %copy.42, f32[128,20]{0,1:T(8,128)S(1)} %fusion.34), kind=kOutput, calls=%fused_computation.74 | convolution fusion | flops 385638400 | bytes 2734080 | tf_op jit(solution)/shard_map/the,thd->hed/dot_general | solution.py:121
  112.9 1.3 collective-permute-start.1
  114.2 3.0 %collective-permute-start = (bf16[1,1,32,2240]{3,2,1,0:T(8,128)(2,1)S(1)}, bf16[1,1,32,2240]{3,2,1,0:T(8,128)(2,1)S(1)}, u32[]{:S(2)}, u32[]{:S(2)}) collective-permute-start(bf16[1,1,32,2240]{3,2,1,0:T(8,128)(2,1)S(1)} %get-tuple-element.171), channel_id=1, source_target_pairs={{0,1},{2,3},{4,5},{6,7},{8,9},{10,11},{12,13},{14,15},{16,17},{18,... | collective-permute-start | bytes 430088 | tf_op jit(solution)/shard_map/ppermute | solution.py:15
  117.3 1.0 collective-permute-done
  118.6 1.1 fusion.23
  120.0 0.7 pad_maximum_fusion.4
  120.7 6.0 %reduce-scatter.9.cloned.1.call-done = f32[10,112,112]{2,1,0:T(8,128)} async-done(((f32[20,112,112]{2,1,0:T(8,128)}), f32[10,112,112]{2,1,0:T(8,128)}) %reduce-scatter.9.cloned.1.call-update) | async-done | bytes 501776 | tf_op jit(solution)/shard_map/reduce_scatter | solution.py:124
  126.8 1.8 convert_element_type.134
  128.7 1.3 collective-permute-start.3
  130.0 3.7 %collective-permute-start.2 = (bf16[1,1,32,2240]{3,2,1,0:T(8,128)(2,1)S(1)}, bf16[1,1,32,2240]{3,2,1,0:T(8,128)(2,1)}, u32[]{:S(2)}, u32[]{:S(2)}) collective-permute-start(bf16[1,1,32,2240]{3,2,1,0:T(8,128)(2,1)S(1)} %get-tuple-element.169), channel_id=1, source_target_pairs={{0,1},{2,3},{4,5},{6,7},{8,9},{10,11},{12,13},{14,15},{16,17},{18,... | collective-permute-start | bytes 430088 | tf_op jit(solution)/shard_map/ppermute | solution.py:15
  133.7 0.8 slice_reduce_fusion.8
  134.5 0.7 copy-done.18
  135.2 1.5 select_maximum_fusion
  136.7 11.9 %all-reduce.9.cloned.1.call-done = f32[3,3,2240]{2,1,0:T(4,128)} async-done(((f32[3,3,2240]{2,1,0:T(4,128)}), f32[3,3,2240]{2,1,0:T(4,128)}) %all-reduce.9.cloned.1.call-update) | async-done | bytes 80656 | tf_op jit(solution)/shard_map/psum | solution.py:164
  148.7 0.6 reshape.87
  149.3 1.1 add.147
  150.4 2.9 %all_gather.40 = f32[20,112,112]{2,1,0:T(8,128)S(1)} all-gather(f32[10,112,112]{2,1,0:T(8,128)S(1)} %add.147), channel_id=1, replica_groups=mesh['groups'=2,'tm'=8,'space'=2] {'space'}, dimensions={0}, use_global_device_ids=true | all-gather | bytes 1505280 | tf_op jit(solution)/shard_map/all_gather | solution.py:106
  153.4 2.7 multiply_reduce_fusion
  156.1 2.9 %copy.41 = f32[128,20,112]{2,1,0:T(8,128)} copy(f32[128,20,112]{0,2,1:T(8,128)} %get-tuple-element.174) | data formatting | bytes 2293760 | tf_op jit(solution)/shard_map/div | solution.py:112
  159.0 2.8 reshape.73
  161.8 0.7 negate_divide_fusion
  162.5 1.0 fusion.35
  163.5 2.8 fusion.1
  166.3 2.2 collective-permute-start.5
  168.5 3.3 %fusion.15 = bf16[1,4,32,2240]{3,2,1,0:T(8,128)(2,1)} fusion(f32[1,4,32,2240]{3,2,1,0:T(8,128)} %reshape.73, bf16[1,4,32,2240]{3,2,1,0:T(8,128)(2,1)S(1)} %copy-done, bf16[1,1,32,2240]{3,2,1,0:T(8,128)(2,1)S(1)} %collective-permute-done.1, bf16[1,1,32,2240]{3,2,1,0:T(8,128)(2,1)} %copy-done.13, f32[2240]{0:T(1024)} %get-tuple-element.143, ...), kind=kLoop, calls=%fused_computation.42 | loop fusion | flops 8601600 | bytes 6101760 | tf_op jit(solution)/shard_map/convert_element_type | solution.py:113
  171.9 1.4 fusion.5
  173.7 1.4 reshape.75
  175.3 28.4 %all-gather.6 = bf16[8,10,112]{2,1,0:T(8,128)(2,1)S(1)} all-gather(bf16[1,10,112]{2,1,0:T(8,128)(2,1)S(1)} %fusion.39), channel_id=5, replica_groups=mesh['groups'=2,'tm'=8,'space'=2] {'tm'}, dimensions={0}, use_global_device_ids=true | all-gather | bytes 20160 | tf_op jit(solution)/shard_map/all_gather | solution.py:41
  203.7 5.6 %while.27 = (s32[]{:T(128)}, f32[10,112,112]{2,1,0:T(8,128)S(1)}, f32[10,112]{1,0:T(8,128)S(1)}, s32[]{:T(128)}, bf16[8,10,112,112]{3,2,1,0:T(8,128)(2,1)}, /*in...) while((s32[]{:T(128)}, f32[10,112,112]{2,1,0:T(8,128)S(1)}, ...), condition=%wide.region_9.10_spmd, body=%wide.region_8.9_spmd.sunk | while | flops 253126 | bytes 1265763 | solution.py:56
  203.8 1.1 convert_add_fusion.4
  204.9 1.1 convert_add_fusion.4
  206.0 1.1 convert_add_fusion.4
  207.1 1.1 convert_add_fusion.4
  208.2 1.1 convert_add_fusion.4
  209.4 2.3 all_gather.46
  211.8 1.9 all-gather.7
  213.7 1.4 convolution_bitcast_fusion
  215.1 1.3 fusion.3
  216.4 1.5 copy.47
  217.9 1.4 reshape.76
  219.3 1.8 copy.50
  221.1 1.4 reshape.77
  222.6 3.1 %select_convert_fusion = (bf16[1,4,32,2240]{3,2,1,0:T(8,128)(2,1)}, bf16[1,4,32,2240]{3,2,1,0:T(8,128)(2,1)}) fusion(bf16[1,4,32,2240]{3,2,1,0:T(8,128)(2,1)} %reshape.76, bf16[1,4,32,2240]{3,2,1,0:T(8,128)(2,1)} %param.10, bf16[1,4,32,2240]{3,2,1,0:T(8,128)(2,1)} %reshape.75, bf16[1,4,32,2240]{3,2,1,0:T(8,128)(2,1)} %param.9), kind=kLoop, calls=%fused_computation.59 | loop fusion | flops 2007040 | bytes 3440640 | tf_op jit(solution)/shard_map/convert_element_type | solution.py:151
  225.7 2.7 fusion.22
  228.4 46.1 %all-reduce.11.cloned.1.call-done = f32[3,3,2240]{2,1,0:T(4,128)} async-done(((f32[3,3,2240]{2,1,0:T(4,128)}), f32[3,3,2240]{2,1,0:T(4,128)}) %all-reduce.11.cloned.1.call-update) | async-done | bytes 80656 | tf_op jit(solution)/shard_map/psum | solution.py:165
  274.6 1.6 copy.84
  (140 shorter events, 4.4 us)
Async XLA Ops:
  7.2 16.2 %reduce-scatter.7.cloned.1.call-start = ((), (), s32[]{:S(2)}) async-start(), calls=%async_computation.2 | async-start | bytes 1720320 | tf_op jit(solution)/shard_map/reduce_scatter | solution.py:96
  8.3 1.3 copy-start
  9.6 1.3 copy-start.4
  10.9 0.8 copy-start.6
  13.2 10.3 %copy-start.3 = (bf16[1,4,32,2240]{3,2,1,0:T(8,128)(2,1)S(1)}, bf16[1,4,32,2240]{3,2,1,0:T(8,128)(2,1)}, u32[]{:S(2)}) copy-start(bf16[1,4,32,2240]{3,2,1,0:T(8,128)(2,1)} %param.10) | copy-start | bytes 1720324
  13.2 15.4 %copy-start.11 = (bf16[1,4,32,2240]{3,2,1,0:T(8,128)(2,1)S(1)}, bf16[1,4,32,2240]{3,2,1,0:T(8,128)(2,1)}, u32[]{:S(2)}) copy-start(bf16[1,4,32,2240]{3,2,1,0:T(8,128)(2,1)} %param.9) | copy-start | bytes 1720324
  13.2 91.0 %all-gather.11.cloned.1.call-start = ((), (), s32[]{:S(2)}) async-start(), calls=%async_computation.6 | async-start | bytes 5160960 | tf_op jit(solution)/shard_map/all_gather | solution.py:25
  23.4 5.3 %copy-start.1 = (bf16[1,4,32,2240]{3,2,1,0:T(8,128)(2,1)S(1)}, bf16[1,4,32,2240]{3,2,1,0:T(8,128)(2,1)}, u32[]{:S(2)}) copy-start(bf16[1,4,32,2240]{3,2,1,0:T(8,128)(2,1)} %param.12) | copy-start | bytes 1720324
  23.4 103.3 %reduce-scatter.9.cloned.1.call-start = ((), (), s32[]{:S(2)}) async-start(), calls=%async_computation.3 | async-start | bytes 1720320 | tf_op jit(solution)/shard_map/reduce_scatter | solution.py:124
  26.4 9.1 %collective-permute-start.4 = (f32[6,112]{1,0:T(8,128)S(1)}, f32[6,112]{1,0:T(8,128)S(1)}, u32[]{:S(2)}, u32[]{:S(2)}) collective-permute-start(f32[6,112]{1,0:T(8,128)S(1)} %slice.158), channel_id=1, source_target_pairs={{0,1},{2,3},{4,5},{6,7},{8,9},{10,11},{12,13},{14,15},{16,17},{18,... | collective-permute-start | bytes 8072
  29.5 1.5 copy-start.38
  35.5 73.7 %copy-start.8 = (bf16[128,20,112]{0,2,1:T(8,128)(2,1)}, bf16[128,20,112]{0,2,1:T(8,128)(2,1)S(1)}, u32[]{:S(2)}) copy-start(bf16[128,20,112]{0,2,1:T(8,128)(2,1)S(1)} %copy.40) | copy-start | bytes 1720324
  109.1 3.7 %copy-start.28 = (f32[20,1,128]{2,1,0:T(1,128)}, f32[20,1,128]{2,1,0:T(1,128)S(1)}, u32[]{:S(2)}) copy-start(f32[20,1,128]{2,1,0:T(1,128)S(1)} %fusion.44) | copy-start | bytes 30724
  109.2 3.6 %copy-start.35 = (f32[128,20]{0,1:T(8,128)}, f32[128,20]{0,1:T(8,128)S(1)}, u32[]{:S(2)}) copy-start(f32[128,20]{0,1:T(8,128)S(1)} %fusion.34) | copy-start | bytes 30724
  112.8 35.8 %all-reduce.9.cloned.1.call-start = ((), (), s32[]{:S(2)}) async-start(), calls=%async_computation.4 | async-start | bytes 221184 | tf_op jit(solution)/shard_map/psum | solution.py:164
  112.9 4.4 %collective-permute-start.1 = (bf16[1,1,32,2240]{3,2,1,0:T(8,128)(2,1)S(1)}, bf16[1,1,32,2240]{3,2,1,0:T(8,128)(2,1)S(1)}, u32[]{:S(2)}, u32[]{:S(2)}) collective-permute-start(bf16[1,1,32,2240]{3,2,1,0:T(8,128)(2,1)S(1)} %get-tuple-element.172), channel_id=1, source_target_pairs={{1,0},{3,2},{5,4},{7,6},{9,8},{11,10},{13,12},{15,14},{17,16},{19,... | collective-permute-start | bytes 430088 | tf_op jit(solution)/shard_map/ppermute | solution.py:18
  114.2 4.0 %collective-permute-start = (bf16[1,1,32,2240]{3,2,1,0:T(8,128)(2,1)S(1)}, bf16[1,1,32,2240]{3,2,1,0:T(8,128)(2,1)S(1)}, u32[]{:S(2)}, u32[]{:S(2)}) collective-permute-start(bf16[1,1,32,2240]{3,2,1,0:T(8,128)(2,1)S(1)} %get-tuple-element.171), channel_id=1, source_target_pairs={{0,1},{2,3},{4,5},{6,7},{8,9},{10,11},{12,13},{14,15},{16,17},{18,... | collective-permute-start | bytes 430088 | tf_op jit(solution)/shard_map/ppermute | solution.py:15
  118.2 1.5 copy-start.13
  119.8 13.9 %copy-start.29 = (f32[3,3,2240]{2,1,0:T(4,128)S(1)}, f32[3,3,2240]{2,1,0:T(4,128)}, u32[]{:S(2)}) copy-start(f32[3,3,2240]{2,1,0:T(4,128)} %param.13) | copy-start | bytes 241924
  120.7 83.0 %all-gather.13.cloned.1.call-start = ((), (), s32[]{:S(2)}) async-start(), calls=%async_computation.7 | async-start | bytes 2580480 | tf_op jit(solution)/shard_map/all_gather | solution.py:41
  128.6 146.0 %all-reduce.11.cloned.1.call-start = ((), (), s32[]{:S(2)}) async-start(), calls=%async_computation.5 | async-start | bytes 221184 | tf_op jit(solution)/shard_map/psum | solution.py:165
  128.7 5.8 %collective-permute-start.3 = (bf16[1,1,32,2240]{3,2,1,0:T(8,128)(2,1)S(1)}, bf16[1,1,32,2240]{3,2,1,0:T(8,128)(2,1)S(1)}, u32[]{:S(2)}, u32[]{:S(2)}) collective-permute-start(bf16[1,1,32,2240]{3,2,1,0:T(8,128)(2,1)S(1)} %get-tuple-element.170), channel_id=1, source_target_pairs={{1,0},{3,2},{5,4},{7,6},{9,8},{11,10},{13,12},{15,14},{17,16},{19,... | collective-permute-start | bytes 430088 | tf_op jit(solution)/shard_map/ppermute | solution.py:18
  130.0 5.2 %collective-permute-start.2 = (bf16[1,1,32,2240]{3,2,1,0:T(8,128)(2,1)S(1)}, bf16[1,1,32,2240]{3,2,1,0:T(8,128)(2,1)}, u32[]{:S(2)}, u32[]{:S(2)}) collective-permute-start(bf16[1,1,32,2240]{3,2,1,0:T(8,128)(2,1)S(1)} %get-tuple-element.169), channel_id=1, source_target_pairs={{0,1},{2,3},{4,5},{6,7},{8,9},{10,11},{12,13},{14,15},{16,17},{18,... | collective-permute-start | bytes 430088 | tf_op jit(solution)/shard_map/ppermute | solution.py:15
  134.5 0.7 copy-start.18
  149.3 4.1 %copy-start.36 = (f32[128,20]{0,1:T(8,128)S(1)}, f32[128,20]{0,1:T(8,128)}, u32[]{:S(2)}) copy-start(f32[128,20]{0,1:T(8,128)} %copy-done.35) | copy-start | bytes 30724
  150.4 3.0 %copy-start.9 = (bf16[128,20,112]{0,2,1:T(8,128)(2,1)S(1)}, bf16[128,20,112]{0,2,1:T(8,128)(2,1)}, u32[]{:S(2)}) copy-start(bf16[128,20,112]{0,2,1:T(8,128)(2,1)} %copy-done.8) | copy-start | bytes 1720324
  150.4 3.0 %copy-start.16 = (f32[128,20,112]{0,2,1:T(8,128)S(1)}, f32[128,20,112]{0,2,1:T(8,128)}, u32[]{:S(2)}) copy-start(f32[128,20,112]{0,2,1:T(8,128)} %copy.42) | copy-start | bytes 3440644
  153.4 2.7 copy-start.14
  159.0 9.4 %copy-start.20 = (f32[2240]{0:T(1024)S(1)}, f32[2240]{0:T(1024)}, u32[]{:S(2)}) copy-start(f32[2240]{0:T(1024)} %get-tuple-element.137) | copy-start | bytes 26884
  162.5 1.0 copy-start.32
  166.3 5.6 %copy-start.30 = (f32[16,112]{1,0:T(8,128)}, f32[16,112]{1,0:T(8,128)S(1)}, u32[]{:S(2)}) copy-start(f32[16,112]{1,0:T(8,128)S(1)} %fusion.1) | copy-start | bytes 21508
  166.3 8.9 %collective-permute-start.5 = (f32[6,112]{1,0:T(8,128)S(1)}, f32[6,112]{1,0:T(8,128)S(1)}, u32[]{:S(2)}, u32[]{:S(2)}) collective-permute-start(f32[6,112]{1,0:T(8,128)S(1)} %slice.159), channel_id=1, source_target_pairs={{0,1},{2,3},{4,5},{6,7},{8,9},{10,11},{12,13},{14,15},{16,17},{18,... | collective-permute-start | bytes 8072
  168.4 3.4 %copy-start.15 = (f32[20,112,112]{2,1,0:T(8,128)S(1)}, f32[20,112,112]{2,1,0:T(8,128)}, u32[]{:S(2)}) copy-start(f32[20,112,112]{2,1,0:T(8,128)} %copy-done.14) | copy-start | bytes 3010564
  168.5 3.4 %copy-start.17 = (f32[128,20,112]{0,2,1:T(8,128)S(1)}, f32[128,20,112]{0,2,1:T(8,128)}, u32[]{:S(2)}) copy-start(f32[128,20,112]{0,2,1:T(8,128)} %copy.42) | copy-start | bytes 3440644
  168.5 3.4 %copy-start.33 = (f32[128,20]{0,1:T(8,128)S(1)}, f32[128,20]{0,1:T(8,128)}, u32[]{:S(2)}) copy-start(f32[128,20]{0,1:T(8,128)} %copy-done.32) | copy-start | bytes 30724
  168.5 3.4 %copy-start.34 = (f32[20,112]{1,0:T(8,128)S(1)}, f32[20,112]{1,0:T(8,128)}, u32[]{:S(2)}) copy-start(f32[20,112]{1,0:T(8,128)} %reshape.87) | copy-start | bytes 26884
  168.5 3.4 %copy-start.37 = (f32[128,20]{0,1:T(8,128)S(1)}, f32[128,20]{0,1:T(8,128)}, u32[]{:S(2)}) copy-start(f32[128,20]{0,1:T(8,128)} %copy-done.35) | copy-start | bytes 30724
  173.3 1.9 copy-start.31
  203.7 5.6 %copy-start.12 = (f32[10,112,112]{2,1,0:T(8,128)S(1)}, f32[10,112,112]{2,1,0:T(8,128)}, u32[]{:S(2)}) copy-start(f32[10,112,112]{2,1,0:T(8,128)} %reduce-scatter.9.cloned.1.call-done) | copy-start | bytes 1505284
  209.3 4.4 %copy-start.5 = (bf16[128,20,112]{0,2,1:T(8,128)(2,1)S(1)}, bf16[128,20,112]{0,2,1:T(8,128)(2,1)}, u32[]{:S(2)}) copy-start(bf16[128,20,112]{0,2,1:T(8,128)(2,1)} %copy-done.4) | copy-start | bytes 1720324
  211.8 3.4 %copy-start.7 = (bf16[128,20,112]{0,2,1:T(8,128)(2,1)S(1)}, bf16[128,20,112]{0,2,1:T(8,128)(2,1)}, u32[]{:S(2)}) copy-start(bf16[128,20,112]{0,2,1:T(8,128)(2,1)} %copy-done.6) | copy-start | bytes 1720324
  222.5 3.2 %copy-start.2 = (bf16[1,4,32,2240]{3,2,1,0:T(8,128)(2,1)S(1)}, bf16[1,4,32,2240]{3,2,1,0:T(8,128)(2,1)}, u32[]{:S(2)}) copy-start(bf16[1,4,32,2240]{3,2,1,0:T(8,128)(2,1)} %param.12) | copy-start | bytes 1720324
  222.5 3.2 %copy-start.10 = (f32[1,4,32,2240]{3,2,1,0:T(8,128)S(1)}, f32[1,4,32,2240]{3,2,1,0:T(8,128)}, u32[]{:S(2)}) copy-start(f32[1,4,32,2240]{3,2,1,0:T(8,128)} %reshape.77) | copy-start | bytes 3440644
  222.5 3.2 %copy-start.19 = (bf16[1,1,32,2240]{3,2,1,0:T(8,128)(2,1)S(1)}, bf16[1,1,32,2240]{3,2,1,0:T(8,128)(2,1)}, u32[]{:S(2)}) copy-start(bf16[1,1,32,2240]{3,2,1,0:T(8,128)(2,1)} %copy-done.18) | copy-start | bytes 430084
  222.5 3.2 %copy-start.21 = (f32[2240]{0:T(1024)S(1)}, f32[2240]{0:T(1024)}, u32[]{:S(2)}) copy-start(f32[2240]{0:T(1024)} %get-tuple-element.138) | copy-start | bytes 26884
  222.5 3.2 %copy-start.22 = (f32[2240]{0:T(1024)S(1)}, f32[2240]{0:T(1024)}, u32[]{:S(2)}) copy-start(f32[2240]{0:T(1024)} %get-tuple-element.139) | copy-start | bytes 26884
  222.5 3.2 %copy-start.23 = (f32[2240]{0:T(1024)S(1)}, f32[2240]{0:T(1024)}, u32[]{:S(2)}) copy-start(f32[2240]{0:T(1024)} %get-tuple-element.140) | copy-start | bytes 26884
  222.5 3.2 %copy-start.24 = (f32[2240]{0:T(1024)S(1)}, f32[2240]{0:T(1024)}, u32[]{:S(2)}) copy-start(f32[2240]{0:T(1024)} %get-tuple-element.141) | copy-start | bytes 26884
  222.6 3.2 %copy-start.25 = (f32[2240]{0:T(1024)S(1)}, f32[2240]{0:T(1024)}, u32[]{:S(2)}) copy-start(f32[2240]{0:T(1024)} %get-tuple-element.142) | copy-start | bytes 26884
  222.6 3.2 %copy-start.26 = (f32[2240]{0:T(1024)S(1)}, f32[2240]{0:T(1024)}, u32[]{:S(2)}) copy-start(f32[2240]{0:T(1024)} %get-tuple-element.143) | copy-start | bytes 26884
  222.6 3.2 %copy-start.27 = (f32[2240]{0:T(1024)S(1)}, f32[2240]{0:T(1024)}, u32[]{:S(2)}) copy-start(f32[2240]{0:T(1024)} %get-tuple-element.144) | copy-start | bytes 26884
Sparse Core Ops, SparseCore 0:
  13.4 9.9 reduce-scatter.6
  25.6 78.6 all-gather.10
  113.0 13.7 reduce-scatter.8
  129.5 19.0 all-reduce.8
  150.7 52.2 all-gather.12
  206.2 68.3 all-reduce.10
